TPU v7x, 32 devices: a whole 2x2x4 slice. The times are simulated.
32 devices in a mesh: dp: 8 (over z, x), tensor: 4 (over y, core).
Axes of the slice: x: 2, y: 2, z: 4, core: 2. Of those that a mesh axis runs over, the one named last changes fastest.
Arguments:
- images: bfloat16 [16, 197, 768], P('dp'), may hold values from -6 to 6
- image_counts: int32 [8], P('dp'), may hold values from 1 to 2, as said below
- first_norm_gain: float32 [768], replicated, may hold values from 0.5 to 1.5
- first_norm_bias: float32 [768], replicated, may hold values from -3 to 3
- qkv_weight: bfloat16 [768, 3, 768], P(None, None, 'tensor'), may hold values from -2 to 2
- qv_bias: float32 [2, 768], P(None, 'tensor'), may hold values from -3 to 3
- out_weight: bfloat16 [768, 768], P('tensor'), may hold values from -1.25 to 1.25
- out_bias: float32 [768], replicated, may hold values from -3 to 3
- second_norm_gain: float32 [768], replicated, may hold values from 0.5 to 1.5
- second_norm_bias: float32 [768], replicated, may hold values from -3 to 3
- fc1_weight: bfloat16 [768, 3072], P(None, 'tensor'), may hold values from -0.21875 to 0.21875
- fc1_bias: float32 [3072], P('tensor'), may hold values from -3 to 3
- fc2_weight: bfloat16 [3072, 768], P('tensor'), may hold values from -0.15625 to 0.15625
- fc2_bias: float32 [768], replicated, may hold values from -3 to 3
- cotangent: bfloat16 [16, 197, 768], P('dp'), may hold values from -6 to 6
Outputs:
- block_out: bfloat16 [16, 197, 768], P('dp')
- input_grad: bfloat16 [16, 197, 768], P('dp')
- grad_first_norm_gain: float32 [768], replicated
- grad_first_norm_bias: float32 [768], replicated
- grad_qkv_weight: float32 [768, 3, 768], P(None, None, 'tensor')
- grad_qv_bias: float32 [2, 768], P(None, 'tensor')
- grad_out_weight: float32 [768, 768], P('tensor')
- grad_out_bias: float32 [768], replicated
- grad_second_norm_gain: float32 [768], replicated
- grad_second_norm_bias: float32 [768], replicated
- grad_fc1_weight: float32 [768, 3072], P(None, 'tensor')
- grad_fc1_bias: float32 [3072], P('tensor')
- grad_fc2_weight: float32 [3072, 768], P('tensor')
- grad_fc2_bias: float32 [768], replicated
Inputs may be any that keep to these rules, and one draw needn't show every extreme that they name: `image_counts`: some index of dp has 2 live slots and some has 1; live slots come first in each index's block of 2.
All inputs are finite; a program needn't handle non-finite values.
Results may differ from a plain program's by a relative error of at most 0.02.
Values may be sent and summed in bfloat16 or wider, within the bound.
A program may use at most 128 MiB of HBM per device.

v0:
```python
import jax
import jax.numpy as jnp
from jax import lax
from jax.sharding import PartitionSpec as P

HEAD_DIM = 64


EPS = 1e-06
ROOT_HALF = 0.7071067811865476
INV_ROOT_TAU = 0.3989422804014327


def to_half(array_in):
    return array_in.astype(jnp.bfloat16)


def norm_forward(row_values, gain_vec, shift_vec):
    centre = row_values - jnp.mean(row_values, axis=-1, keepdims=True)
    inverse = lax.rsqrt(jnp.mean(centre * centre, axis=-1, keepdims=True) + EPS)
    scaled = centre * inverse
    return (scaled * gain_vec + shift_vec, scaled, inverse)


def norm_backward(grad_out, scaled, inverse, gain_vec):
    grad_scaled = grad_out * gain_vec
    grad_rows = inverse * (
        grad_scaled
        - jnp.mean(grad_scaled, axis=-1, keepdims=True)
        - scaled * jnp.mean(grad_scaled * scaled, axis=-1, keepdims=True)
    )
    return (grad_rows, jnp.sum(grad_out * scaled, axis=0), jnp.sum(grad_out, axis=0))


def gelu_value(pre_act):
    return 0.5 * pre_act * (1.0 + jax.scipy.special.erf(pre_act * ROOT_HALF))


def gelu_slope(pre_act):
    return (
        0.5 * (1.0 + jax.scipy.special.erf(pre_act * ROOT_HALF))
        + pre_act * jnp.exp(-0.5 * pre_act * pre_act) * INV_ROOT_TAU
    )


def per_device(
    images,
    image_counts,
    first_norm_gain,
    first_norm_bias,
    qkv_weight,
    qv_bias,
    out_weight,
    out_bias,
    second_norm_gain,
    second_norm_bias,
    fc1_weight,
    fc1_bias,
    fc2_weight,
    fc2_bias,
    cotangent,
):
    f32 = jnp.float32
    slot_count, length, model_width = images.shape
    local_width = qkv_weight.shape[2]
    local_heads = local_width // HEAD_DIM
    row_count = slot_count * length
    score_scale = HEAD_DIM ** (-0.5)
    live_slots = (jnp.arange(slot_count, dtype=jnp.int32) < image_counts[0]).astype(f32)
    row_live = jnp.broadcast_to(live_slots[:, None], (slot_count, length)).reshape(row_count, 1)
    head_shape = (slot_count, length, local_heads, HEAD_DIM)
    row_values = images.reshape(row_count, model_width).astype(f32)
    norm_one, scaled_one, inverse_one = norm_forward(row_values, first_norm_gain, first_norm_bias)
    norm_one = to_half(norm_one)
    qkv_flat = qkv_weight.reshape(model_width, 3 * local_width)
    qkv_shift = jnp.stack([qv_bias[0], jnp.zeros_like(qv_bias[0]), qv_bias[1]])
    qkv_rows = to_half(
        jnp.dot(norm_one, qkv_flat, preferred_element_type=f32).reshape(row_count, 3, local_width)
        + qkv_shift
    )
    queries = qkv_rows[:, 0].reshape(head_shape)
    key_heads = qkv_rows[:, 1].reshape(head_shape)
    value_heads = qkv_rows[:, 2].reshape(head_shape)
    scores = (
        jnp.einsum("bqhd,bkhd->bhqk", queries, key_heads, preferred_element_type=f32) * score_scale
    )
    row_peak = jnp.max(scores, axis=-1, keepdims=True)
    log_total = row_peak + jnp.log(jnp.sum(jnp.exp(scores - row_peak), axis=-1, keepdims=True))
    probs_full = jnp.exp(scores - log_total)
    probs_half = to_half(probs_full)
    context = to_half(
        jnp.einsum("bhqk,bkhd->bqhd", probs_half, value_heads, preferred_element_type=f32)
    )
    context_rows = context.reshape(row_count, local_width)
    attn_part = jnp.dot(context_rows, out_weight, preferred_element_type=f32)
    resid_rows = (
        row_values
        + lax.psum(attn_part.astype(jnp.bfloat16), "tensor").astype(jnp.float32)
        + out_bias
    )
    norm_two, scaled_two, inverse_two = norm_forward(resid_rows, second_norm_gain, second_norm_bias)
    norm_two = to_half(norm_two)
    pre_act = jnp.dot(norm_two, fc1_weight, preferred_element_type=f32) + fc1_bias
    act_half = to_half(gelu_value(pre_act))
    mlp_part = jnp.dot(act_half, fc2_weight, preferred_element_type=f32)
    final_rows = (
        resid_rows
        + lax.psum(mlp_part.astype(jnp.bfloat16), "tensor").astype(jnp.float32)
        + fc2_bias
    )
    block_out = to_half(final_rows * row_live).reshape(slot_count, length, model_width)
    inv_images = 1.0 / (slot_count * lax.axis_size("dp"))
    grad_final = cotangent.reshape(row_count, model_width).astype(f32) * row_live
    grad_final_half = to_half(grad_final)
    grad_act = jnp.dot(grad_final_half, fc2_weight.T, preferred_element_type=f32)
    grad_pre = grad_act * gelu_slope(pre_act)
    grad_pre_half = to_half(grad_pre)
    two_part = jnp.dot(grad_pre_half, fc1_weight.T, preferred_element_type=f32)
    grad_norm_two = lax.psum(two_part.astype(jnp.bfloat16), "tensor").astype(jnp.float32)
    back_two, gain_two, shift_two = norm_backward(
        grad_norm_two, scaled_two, inverse_two, second_norm_gain
    )
    mlp_grads = (
        jnp.dot(norm_two.T, grad_pre_half, preferred_element_type=f32) * inv_images,
        jnp.sum(grad_pre, axis=0, keepdims=True) * inv_images,
        jnp.dot(act_half.T, grad_final_half, preferred_element_type=f32) * inv_images,
        jnp.stack([gain_two, shift_two, jnp.sum(grad_final, axis=0)]) * inv_images,
    )
    grad_resid = grad_final + back_two
    grad_resid_half = to_half(grad_resid)
    grad_context = to_half(
        jnp.dot(grad_resid_half, out_weight.T, preferred_element_type=f32)
    ).reshape(head_shape)
    grad_probs = jnp.einsum(
        "bqhd,bkhd->bhqk", grad_context, value_heads, preferred_element_type=f32
    )
    grad_scores = to_half(
        probs_full
        * (grad_probs - jnp.sum(probs_full * grad_probs, axis=-1, keepdims=True))
        * score_scale
    )
    grad_queries = jnp.einsum(
        "bhqk,bkhd->bqhd", grad_scores, key_heads, preferred_element_type=f32
    ).reshape(row_count, local_width)
    grad_keys = jnp.einsum(
        "bhqk,bqhd->bkhd", grad_scores, queries, preferred_element_type=f32
    ).reshape(row_count, local_width)
    grad_values = jnp.einsum(
        "bhqk,bqhd->bkhd", probs_half, grad_context, preferred_element_type=f32
    ).reshape(row_count, local_width)
    grad_qkv_half = to_half(jnp.stack([grad_queries, grad_keys, grad_values], axis=1)).reshape(
        row_count, 3 * local_width
    )
    one_part = jnp.dot(grad_qkv_half, qkv_flat.T, preferred_element_type=f32)
    grad_norm_one = lax.psum(one_part.astype(jnp.bfloat16), "tensor").astype(jnp.float32)
    back_one, gain_one, shift_one = norm_backward(
        grad_norm_one, scaled_one, inverse_one, first_norm_gain
    )
    input_grad = to_half(grad_resid + back_one).reshape(slot_count, length, model_width)
    attn_grads = (
        jnp.dot(norm_one.T, grad_qkv_half, preferred_element_type=f32) * inv_images,
        jnp.stack([jnp.sum(grad_queries, axis=0), jnp.sum(grad_values, axis=0)]) * inv_images,
        jnp.dot(context_rows.T, grad_resid_half, preferred_element_type=f32) * inv_images,
        jnp.stack([gain_one, shift_one, jnp.sum(grad_resid, axis=0)]) * inv_images,
    )
    shares = (
        lax.psum_scatter(attn_grads[0], "dp", scatter_dimension=1, tiled=True),
        lax.psum_scatter(attn_grads[1], "dp", scatter_dimension=1, tiled=True),
        lax.psum_scatter(attn_grads[2], "dp", scatter_dimension=1, tiled=True),
        lax.psum_scatter(attn_grads[3], "dp", scatter_dimension=1, tiled=True),
        lax.psum_scatter(mlp_grads[0], "dp", scatter_dimension=1, tiled=True),
        lax.psum_scatter(mlp_grads[1], "dp", scatter_dimension=1, tiled=True),
        lax.psum_scatter(mlp_grads[2], "dp", scatter_dimension=1, tiled=True),
        lax.psum_scatter(mlp_grads[3], "dp", scatter_dimension=1, tiled=True),
    )
    gathered = (
        lax.all_gather(shares[0].astype(jnp.bfloat16), "dp", axis=1, tiled=True).astype(
            jnp.float32
        ),
        lax.all_gather(shares[1].astype(jnp.bfloat16), "dp", axis=1, tiled=True).astype(
            jnp.float32
        ),
        lax.all_gather(shares[2].astype(jnp.bfloat16), "dp", axis=1, tiled=True).astype(
            jnp.float32
        ),
        lax.all_gather(shares[3].astype(jnp.bfloat16), "dp", axis=1, tiled=True).astype(
            jnp.float32
        ),
        lax.all_gather(shares[4].astype(jnp.bfloat16), "dp", axis=1, tiled=True).astype(
            jnp.float32
        ),
        lax.all_gather(shares[5].astype(jnp.bfloat16), "dp", axis=1, tiled=True).astype(
            jnp.float32
        ),
        lax.all_gather(shares[6].astype(jnp.bfloat16), "dp", axis=1, tiled=True).astype(
            jnp.float32
        ),
        lax.all_gather(shares[7].astype(jnp.bfloat16), "dp", axis=1, tiled=True).astype(
            jnp.float32
        ),
    )
    attn_full = gathered[:4]
    mlp_full = gathered[4:]
    return (
        block_out,
        input_grad,
        attn_full[3][0],
        attn_full[3][1],
        attn_full[0].reshape(model_width, 3, local_width),
        attn_full[1],
        attn_full[2],
        attn_full[3][2],
        mlp_full[3][0],
        mlp_full[3][1],
        mlp_full[0],
        mlp_full[1][0],
        mlp_full[2],
        mlp_full[3][2],
    )


def solution(mesh):
    placed = (
        P("dp", None, None),
        P("dp"),
        P(),
        P(),
        P(None, None, "tensor"),
        P(None, "tensor"),
        P("tensor", None),
        P(),
        P(),
        P(),
        P(None, "tensor"),
        P("tensor"),
        P("tensor", None),
        P(),
        P("dp", None, None),
    )
    return jax.shard_map(
        per_device,
        mesh=mesh,
        in_specs=placed,
        out_specs=(
            P("dp", None, None),
            P("dp", None, None),
            P(),
            P(),
            P(None, None, "tensor"),
            P(None, "tensor"),
            P("tensor", None),
            P(),
            P(),
            P(),
            P(None, "tensor"),
            P("tensor"),
            P("tensor", None),
            P(),
        ),
        check_vma=False,
    )
```

profile of v0, /device:TPU:0, one launch (start us, length us, event | category | flops | bytes accessed | tf_op | source)
XLA Modules:
  0.0 741.2 jit_solution(13153335465204012786)
XLA Ops:
  19.7 2.2 convolution_convert_fusion.2
  25.3 33.3 %all-reduce.7.cloned.1.call-done = bf16[394,768]{1,0:T(8,128)(2,1)} async-done(((bf16[394,768]{1,0:T(8,128)(2,1)}), bf16[394,768]{1,0:T(8,128)(2,1)}) %all-reduce.7.cloned.1.call-update) | async-done | bytes 605200 | tf_op jit(solution)/shard_map/psum | solution.py:98
  66.8 2.9 convolution_convert_fusion.1
  69.7 31.1 %all-reduce.9.cloned.1.call-done = bf16[394,768]{1,0:T(8,128)(2,1)} async-done(((bf16[394,768]{1,0:T(8,128)(2,1)}), bf16[394,768]{1,0:T(8,128)(2,1)}) %all-reduce.9.cloned.1.call-update) | async-done | bytes 605200 | tf_op jit(solution)/shard_map/psum | solution.py:119
  107.8 4.5 fusion.69
  112.3 3.8 fusion.34
  126.7 2.9 fusion.10
  130.3 3.4 convolution_multiply_fusion.1
  137.3 3.6 convolution_multiply_fusion
  142.0 26.2 %all-reduce.11.cloned.1.call-done = (bf16[394,768]{1,0:T(8,128)(2,1)}, bf16[394,768]{1,0:T(8,128)(2,1)}) async-done(((bf16[394,768]{1,0:T(8,128)(2,1)}, bf16[394,768]{1,0:T(8,128)(2,1)}), (bf16[394,768]{1,0:T(8,128)(2,1)}, bf16[394,768]{1,0:T(8,128)(2,1)})) %all-reduce.11.cloned.1.call-update) | async-done | bytes 1210384 | tf_op jit(solution)/shard_map/psum | solution.py:108
  171.4 2.4 convolution_multiply_fusion.5
  173.9 2.3 copy.172
  177.2 3.1 convolution_multiply_fusion.2
  180.4 61.4 %reduce-scatter.19.cloned.1.call-done = f32[768,96]{0,1:T(8,128)} async-done(((f32[768,768]{0,1:T(8,128)}), f32[768,96]{0,1:T(8,128)}) %reduce-scatter.19.cloned.1.call-update) | async-done | bytes 294928 | tf_op jit(solution)/shard_map/reduce_scatter | solution.py:171
  245.3 60.9 %reduce-scatter.29.cloned.1.call-done = f32[96,1]{1,0:T(8,128)} async-done(((f32[768,1]{1,0:T(8,128)}), f32[96,1]{1,0:T(8,128)}) %reduce-scatter.29.cloned.1.call-update) | async-done | bytes 400
  307.3 19.5 %all-reduce = bf16[768]{0:T(1024)(128)(2,1)S(1)} all-reduce(bf16[768]{0:T(1024)(128)(2,1)S(1)} %dynamic-update-slice), channel_id=1, replica_groups=mesh['dp'=8,'tensor'=4] {'dp'}, use_global_device_ids=true, to_apply=%add | all-reduce | flops 768 | bytes 3072
  327.6 17.2 %all-reduce.1 = bf16[2,192]{1,0:T(2,128)(2,1)S(1)} all-reduce(f32[2,192]{1,0:T(2,128)S(1)} %maximum_multiply_fusion.2), channel_id=4, replica_groups=mesh['dp'=8,'tensor'=4] {'dp'}, use_global_device_ids=true, to_apply=%region_22.0.clone | all-reduce | flops 384 | bytes 2304
  344.8 18.3 %all-gather.1 = bf16[8,24,2]{1,2,0:T(2,128)(2,1)S(1)} all-gather(bf16[1,24,2]{1,2,0:T(2,128)(2,1)S(1)} %fusion.60), channel_id=1, replica_groups=mesh['dp'=8,'tensor'=4] {'dp'}, dimensions={0}, use_global_device_ids=true | all-gather | bytes 864 | tf_op jit(solution)/shard_map/all_gather | solution.py:180
  363.8 7.4 %reduce-scatter.27.cloned.1.call-done = f32[96,3]{1,0:T(8,128)} async-done(((f32[768,3]{1,0:T(8,128)}), f32[96,3]{1,0:T(8,128)}) %reduce-scatter.27.cloned.1.call-update) | async-done | bytes 1168
  372.1 19.0 %all-gather.2 = bf16[8,96,3]{1,2,0:T(4,128)(2,1)S(1)} all-gather(bf16[1,96,3]{1,2,0:T(4,128)(2,1)S(1)} %bitcast.107), channel_id=1, replica_groups=mesh['dp'=8,'tensor'=4] {'dp'}, dimensions={0}, use_global_device_ids=true | all-gather | bytes 5184 | tf_op jit(solution)/shard_map/all_gather | solution.py:198
  391.1 52.8 %reduce-scatter.21.cloned.1.call-done = f32[768,96]{0,1:T(8,128)} async-done(((f32[768,768]{0,1:T(8,128)}), f32[768,96]{0,1:T(8,128)}) %reduce-scatter.21.cloned.1.call-update) | async-done | bytes 294928 | tf_op jit(solution)/shard_map/reduce_scatter | solution.py:173
  450.6 2.5 copy.159
  456.9 51.7 %reduce-scatter.23.cloned.1.call-done = f32[96,3]{1,0:T(8,128)} async-done(((f32[768,3]{1,0:T(8,128)}), f32[96,3]{1,0:T(8,128)}) %reduce-scatter.23.cloned.1.call-update) | async-done | bytes 1168
  509.4 18.7 %all-gather = bf16[8,96,3]{1,2,0:T(4,128)(2,1)S(1)} all-gather(bf16[1,96,3]{1,2,0:T(4,128)(2,1)S(1)} %bitcast.108), channel_id=1, replica_groups=mesh['dp'=8,'tensor'=4] {'dp'}, dimensions={0}, use_global_device_ids=true | all-gather | bytes 5184 | tf_op jit(solution)/shard_map/all_gather | solution.py:186
  528.8 45.3 %reduce-scatter.25.cloned.1.call-done = f32[96,192]{1,0:T(8,128)} async-done(((f32[768,192]{1,0:T(8,128)}), f32[96,192]{1,0:T(8,128)}) %reduce-scatter.25.cloned.1.call-update) | async-done | bytes 73744
  575.2 31.8 %all_gather.27 = bf16[192,768]{0,1:T(8,128)(2,1)S(1)} all-gather(bf16[192,96]{0,1:T(8,128)(2,1)S(1)} %copy.157), channel_id=1, replica_groups=mesh['dp'=8,'tensor'=4] {'dp'}, dimensions={1}, use_global_device_ids=true | all-gather | bytes 331776 | tf_op jit(solution)/shard_map/all_gather | solution.py:183
  608.0 36.5 %reduce-scatter.17.cloned.1.call-done = f32[768,72]{0,1:T(8,128)} async-done(((f32[768,576]{0,1:T(8,128)}), f32[768,72]{0,1:T(8,128)}) %reduce-scatter.17.cloned.1.call-update) | async-done | bytes 221200 | tf_op jit(solution)/shard_map/reduce_scatter | solution.py:167
  645.4 33.5 %all_gather.25 = bf16[768,576]{0,1:T(8,128)(2,1)S(1)} all-gather(bf16[768,72]{0,1:T(8,128)(2,1)S(1)} %convert_element_type.185), channel_id=1, replica_groups=mesh['dp'=8,'tensor'=4] {'dp'}, dimensions={1}, use_global_device_ids=true | all-gather | bytes 995328 | tf_op jit(solution)/shard_map/all_gather | solution.py:177
  680.3 8.9 %all-gather.6.cloned.1.call-done = bf16[768,768]{0,1:T(8,128)(2,1)} async-done(((bf16[768,96]{0,1:T(8,128)(2,1)}), bf16[768,768]{0,1:T(8,128)(2,1)}) %all-gather.6.cloned.1.call-update) | async-done | bytes 1179664 | tf_op jit(solution)/shard_map/all_gather | solution.py:189
  689.1 2.7 copy.162
  691.9 39.8 %all-gather.8.cloned.1.call-done = bf16[768,768]{0,1:T(8,128)(2,1)} async-done(((bf16[768,96]{0,1:T(8,128)(2,1)}), bf16[768,768]{0,1:T(8,128)(2,1)}) %all-gather.8.cloned.1.call-update) | async-done | bytes 1179664 | tf_op jit(solution)/shard_map/all_gather | solution.py:195
  731.6 2.7 copy.163
  (204 shorter events, 72.3 us)
Async XLA Ops:
  7.2 53.4 %copy-start = (bf16[768,768]{1,0:T(8,128)(2,1)S(1)}, bf16[768,768]{1,0:T(8,128)(2,1)}, u32[]{:S(2)}) copy-start(bf16[768,768]{1,0:T(8,128)(2,1)} %param.25) | copy-start | bytes 3538948
  7.2 3.0 copy-start.24
  7.2 3.0 copy-start.22
  7.2 51.3 %all-reduce.7.cloned.1.call-start = ((), (), s32[]{:S(2)}) async-start(), calls=%async_computation.7 | async-start | bytes 1228800 | tf_op jit(solution)/shard_map/psum | solution.py:98
  11.6 2.6 copy-start.8
  14.5 2.4 copy-start.18
  19.6 2.3 copy-start.13
  21.9 78.9 %all-reduce.9.cloned.1.call-start = ((), (), s32[]{:S(2)}) async-start(), calls=%async_computation.8 | async-start | bytes 1228800 | tf_op jit(solution)/shard_map/psum | solution.py:119
  23.3 35.3 %copy-start.25 = (f32[768]{0:T(1024)S(1)}, f32[768]{0:T(1024)}, u32[]{:S(2)}) copy-start(f32[768]{0:T(1024)} %param.22) | copy-start | bytes 9220
  25.1 35.1 %copy-start.31 = (f32[2]{0:T(128)}, f32[2]{0:T(128)S(1)}, u32[]{:S(2)}) copy-start(f32[2]{0:T(128)S(1)} %compare_convert_fusion) | copy-start | bytes 28
  66.5 101.7 %all-reduce.11.cloned.1.call-start = ((), (), s32[]{:S(2)}) async-start(), calls=%async_computation.18 | async-start | bytes 2457600 | tf_op jit(solution)/shard_map/psum | solution.py:108
  100.8 1.9 copy-start.6
  100.8 1.9 copy-start.11
  107.8 4.5 copy-start.19
  129.6 112.1 %reduce-scatter.19.cloned.1.call-start = ((), (), s32[]{:S(2)}) async-start(), calls=%async_computation.10 | async-start | bytes 2654208 | tf_op jit(solution)/shard_map/reduce_scatter | solution.py:171
  133.7 172.5 %reduce-scatter.29.cloned.1.call-start = ((), (), s32[]{:S(2)}) async-start(), calls=%async_computation.17 | async-start | bytes 442368
  135.2 2.1 copy-start.20
  136.2 235.0 %reduce-scatter.27.cloned.1.call-start = ((), (), s32[]{:S(2)}) async-start(), calls=%async_computation.16 | async-start | bytes 442368
  137.2 306.7 %reduce-scatter.21.cloned.1.call-start = ((), (), s32[]{:S(2)}) async-start(), calls=%async_computation.12 | async-start | bytes 2654208 | tf_op jit(solution)/shard_map/reduce_scatter | solution.py:173
  140.9 367.6 %reduce-scatter.23.cloned.1.call-start = ((), (), s32[]{:S(2)}) async-start(), calls=%async_computation.14 | async-start | bytes 442368
  168.2 3.2 copy-start.14
  171.4 402.7 %reduce-scatter.25.cloned.1.call-start = ((), (), s32[]{:S(2)}) async-start(), calls=%async_computation.15 | async-start | bytes 884736
  173.9 2.4 copy-start.9
  176.2 468.3 %reduce-scatter.17.cloned.1.call-start = ((), (), s32[]{:S(2)}) async-start(), calls=%async_computation.9 | async-start | bytes 1990656 | tf_op jit(solution)/shard_map/reduce_scatter | solution.py:167
  180.3 63.2 %copy-start.28 = (u32[32]{0:T(128)S(1)}, u32[32]{0:T(128)}, u32[]{:S(2)}) copy-start(u32[32]{0:T(128)} %constant.41) | copy-start | bytes 388
  180.3 147.2 %copy-start.29 = (f32[3,64]{1,0:T(4,128)S(1)}, f32[3,64]{1,0:T(4,128)}, u32[]{:S(2)}) copy-start(f32[3,64]{1,0:T(4,128)} %get-tuple-element.107) | copy-start | bytes 2308
  180.3 266.0 %copy-start.26 = (f32[768]{0:T(1024)S(1)}, f32[768]{0:T(1024)}, u32[]{:S(2)}) copy-start(f32[768]{0:T(1024)} %param.28) | copy-start | bytes 9220
  180.3 508.8 %all-gather.6.cloned.1.call-start = ((), (), s32[]{:S(2)}) async-start(), calls=%async_computation.11 | async-start | bytes 1327104 | tf_op jit(solution)/shard_map/all_gather | solution.py:189
  243.4 488.2 %all-gather.8.cloned.1.call-start = ((), (), s32[]{:S(2)}) async-start(), calls=%async_computation.13 | async-start | bytes 1327104 | tf_op jit(solution)/shard_map/all_gather | solution.py:195
  446.3 6.7 copy-start.10
  448.5 4.6 copy-start.2
  450.6 2.5 copy-start.4
  (18 other events, 20.4 us)
Sparse Core Ops, SparseCore 0:
  22.0 36.4 all-reduce.6
  66.6 34.0 all-reduce.8
  129.7 38.4 all-reduce.10
  172.1 69.5 reduce-scatter.18
  244.8 61.3 reduce-scatter.28
  309.9 61.2 reduce-scatter.26
  375.3 68.6 reduce-scatter.20
  447.2 61.3 reduce-scatter.22
  511.9 62.2 reduce-scatter.24
  578.0 66.4 reduce-scatter.16
  646.7 42.4 all-gather.5
  691.2 40.3 all-gather.7
where the time goes:
time: 743 us; the launch traced here: 741 us
  waiting for transfers between devices  455 us (61%)
  blocking collectives  158 us (21%)
  local copies, waits for them, and re-layouts  47.1 us (6%)
  matrix products  41.1 us (6%)
  other arithmetic  22.2 us (3%)
  between operations  16.8 us (2%)
    unnamed x16, waiting for transfers between devices  166 us
    reduce_scatter x1, waiting for transfers between devices, per_device(): lax.psum_scatter(mlp_grads[0], 'dp', scatter_dimension=1, tiled=True)  61.4 us
    reduce_scatter x1, waiting for transfers between devices, per_device(): lax.psum_scatter(mlp_grads[2], 'dp', scatter_dimension=1, tiled=True)  52.8 us
    all_gather x1, waiting for transfers between devices, per_device(): lax.all_gather(shares[6].astype(jnp.bfloat16), 'dp', axis=1, tiled=True)  39.8 us
    unnamed x2, blocking collectives  36.6 us
    reduce_scatter x1, waiting for transfers between devices, per_device(): lax.psum_scatter(attn_grads[0], 'dp', scatter_dimension=1, tiled=True)  36.5 us
    all_gather x1, blocking collectives, per_device(): lax.all_gather(shares[0].astype(jnp.bfloat16), 'dp', axis=1, tiled=True)  33.5 us
    psum x1, waiting for transfers between devices, per_device(): lax.psum(attn_part.astype(jnp.bfloat16), 'tensor').astype(jnp.float32)  33.3 us
  transfers between devices with their start and end apart: 12, of which 12 were waited for; matrix products, arithmetic and copies ran while one was open for 7% of the time, Pallas kernels for 0%

commit v1 on v0

--- a/solution.py
+++ b/solution.py
@@ -1,6 +1,8 @@
 import jax
 import jax.numpy as jnp
 from jax import lax
+from jax.experimental import pallas as pl
+from jax.experimental.pallas import tpu as pltpu
 from jax.sharding import PartitionSpec as P
 
 HEAD_DIM = 64
@@ -41,6 +43,298 @@
         0.5 * (1.0 + jax.scipy.special.erf(pre_act * ROOT_HALF))
         + pre_act * jnp.exp(-0.5 * pre_act * pre_act) * INV_ROOT_TAU
     )
+
+
+MESH = pl.DeviceIdType.MESH
+ROW_TILE = 16
+
+
+def log2_of(count):
+    steps = count.bit_length() - 1
+    assert 1 << steps == count
+    return steps
+
+
+def bit_of(axis, position):
+    index = lax.axis_index(axis)
+    bit = (index // (1 << position)) % 2
+    return bit, index + (1 - 2 * bit) * (1 << position)
+
+
+def greet(peers):
+    barrier = pltpu.get_barrier_semaphore()
+    for axis, position in peers:
+        _, partner = bit_of(axis, position)
+        pl.semaphore_signal(barrier, inc=1, device_id={axis: partner}, device_id_type=MESH)
+    pl.semaphore_wait(barrier, len(peers))
+
+
+class Wires:
+    def __init__(self, send_sems, recv_sems):
+        self.send_sems, self.recv_sems, self.copies = send_sems, recv_sems, []
+
+    def start(self, source, target, axis, position):
+        _, partner = bit_of(axis, position)
+        slot = len(self.copies)
+        copy = pltpu.make_async_remote_copy(
+            src_ref=source,
+            dst_ref=target,
+            send_sem=self.send_sems.at[slot],
+            recv_sem=self.recv_sems.at[slot],
+            device_id={axis: partner},
+            device_id_type=MESH,
+        )
+        copy.start()
+        self.copies.append(copy)
+        return copy
+
+    def finish(self):
+        for copy in self.copies:
+            copy.wait_send()
+
+
+def run_wavefront(streams):
+    order = sorted(
+        ((place + stage, -stage, place) for place, stages in enumerate(streams) for stage in range(len(stages)))
+    )
+    for _, minus_stage, place in order:
+        streams[place][-minus_stage]()
+
+
+def grad_stages(wires, axis, order, source, landing, result):
+    steps = len(order)
+    count = 1 << steps
+    bits = [bit_of(axis, position)[0] for position in order]
+    held = {}
+
+    def start_halving(step):
+        half = count >> (step + 1)
+        block = source if step == 0 else landing[step - 1]
+        held["copy"] = wires.start(
+            block.at[pl.ds((1 - bits[step]) * half, half)], landing[step], axis, order[step]
+        )
+
+    def start_doubling(step):
+        base = sum(bits[i] * (count >> (i + 1)) for i in range(step + 1))
+        part = result.at[pl.ds(base, count >> (step + 1))]
+        held["copy"] = wires.start(part, part, axis, order[step])
+
+    def add_stage(step):
+        def stage():
+            held["copy"].wait_recv()
+            half = count >> (step + 1)
+            block = source if step == 0 else landing[step - 1]
+            if step < steps - 1:
+                @pl.loop(0, half)
+                def _(i):
+                    mine = block[bits[step] * half + i].astype(jnp.float32)
+                    theirs = landing[step][i].astype(jnp.float32)
+                    landing[step][i] = (mine + theirs).astype(jnp.bfloat16)
+
+                start_halving(step + 1)
+            else:
+                base = sum(bits[i] * (count >> (i + 1)) for i in range(steps))
+                mine = block[bits[step]].astype(jnp.float32)
+                theirs = landing[step][0].astype(jnp.float32)
+                result[base] = (mine + theirs).astype(jnp.bfloat16)
+                start_doubling(steps - 1)
+
+        return stage
+
+    def gather_stage(step):
+        def stage():
+            held["copy"].wait_recv()
+            if step > 0:
+                start_doubling(step - 1)
+
+        return stage
+
+    return (
+        [lambda: start_halving(0)]
+        + [add_stage(step) for step in range(steps)]
+        + [gather_stage(step) for step in reversed(range(steps))]
+    )
+
+
+def vector_stages(wires, axis, steps, source, landing, sums, result):
+    held = {}
+
+    def current(step):
+        return source if step == 0 else sums.at[step - 1]
+
+    def start(step):
+        held["copy"] = wires.start(current(step), landing.at[step], axis, step)
+
+    def stage_of(step):
+        def stage():
+            held["copy"].wait_recv()
+            total = current(step)[...] + landing[step]
+            if step < steps - 1:
+                sums[step] = total
+                start(step + 1)
+            else:
+                result[...] = total
+
+        return stage
+
+    return [lambda: start(0)] + [stage_of(step) for step in range(steps)]
+
+
+def share_stages(wires, axis, steps, source, landing, sums, result, columns):
+    near = bit_of(axis, 0)[0]
+    held = {}
+
+    def start(step):
+        if step == 0:
+            held["copy"] = wires.start(
+                source.at[1 - near, :, columns], landing.at[0, :, columns], axis, 0
+            )
+        else:
+            held["copy"] = wires.start(
+                sums.at[step - 1, :, columns], landing.at[step, :, columns], axis, step
+            )
+
+    def stage_of(step):
+        def stage():
+            held["copy"].wait_recv()
+            mine = source[near, :, columns] if step == 0 else sums[step - 1, :, columns]
+            total = mine.astype(jnp.float32) + landing[step, :, columns].astype(jnp.float32)
+            total = total.astype(jnp.bfloat16)
+            if step < steps - 1:
+                sums[step, :, columns] = total
+                start(step + 1)
+            else:
+                result[near, :, columns] = total
+                part = result.at[near, :, columns]
+                held["copy"] = wires.start(part, part, axis, 0)
+
+        return stage
+
+    return (
+        [lambda: start(0)]
+        + [stage_of(step) for step in range(steps)]
+        + [lambda: held["copy"].wait_recv()]
+    )
+
+
+def column_cuts(width, pieces):
+    size = width // pieces
+    if width % pieces or size % 128:
+        return [slice(0, width)]
+    return [slice(i * size, (i + 1) * size) for i in range(pieces)]
+
+
+VMEM_SPEC = pl.BlockSpec(memory_space=pltpu.VMEM)
+
+
+def tensor_sum(part):
+    rows, width = part.shape
+    steps = log2_of(lax.axis_size("tensor"))
+    cuts = column_cuts(width, 3)
+
+    def kernel(part_ref, out_ref, landing, sums, send_sems, recv_sems):
+        greet([("tensor", position) for position in range(steps)])
+        wires = Wires(send_sems, recv_sems)
+        run_wavefront(
+            [share_stages(wires, "tensor", steps, part_ref, landing, sums, out_ref, cut) for cut in cuts]
+        )
+        wires.finish()
+
+    copies = len(cuts) * (steps + 1)
+    return pl.pallas_call(
+        kernel,
+        out_shape=jax.ShapeDtypeStruct((2, rows // 2, width), jnp.bfloat16),
+        in_specs=[VMEM_SPEC],
+        out_specs=VMEM_SPEC,
+        scratch_shapes=[
+            pltpu.VMEM((steps, rows // 2, width), jnp.bfloat16),
+            pltpu.VMEM((steps, rows // 2, width), jnp.bfloat16),
+            pltpu.SemaphoreType.DMA((copies,)),
+            pltpu.SemaphoreType.DMA((copies,)),
+        ],
+        compiler_params=pltpu.CompilerParams(collective_id=0, has_side_effects=True),
+        name="tensor_sum",
+    )(part.reshape(2, rows // 2, width)).reshape(rows, width)
+
+
+def grad_sum(grads, vectors, part):
+    count = lax.axis_size("dp")
+    steps = log2_of(count)
+    tensor_steps = log2_of(lax.axis_size("tensor"))
+    rows, width = part.shape
+    cuts = column_cuts(width, 3)
+    blocks = []
+    for grad in grads:
+        pieces = 3 if grad.shape[0] % (3 * count * ROW_TILE) == 0 else 1
+        blocks.append(grad.reshape(pieces, count, grad.shape[0] // (pieces * count), grad.shape[1]))
+    total = len(blocks)
+    far_first = [*range(1, steps), 0]
+    near_first = [*range(steps)]
+
+    def kernel(*refs):
+        sources, (vector_ref, part_ref) = refs[:total], refs[total : total + 2]
+        results, (vector_out, part_out) = refs[total + 2 : 2 * total + 2], refs[2 * total + 2 : 2 * total + 4]
+        scratch = refs[2 * total + 4 :]
+        landings = [scratch[i * steps : (i + 1) * steps] for i in range(total)]
+        vector_landing, vector_sums, part_landing, part_sums, send_sems, recv_sems = scratch[total * steps :]
+        greet(
+            [("dp", position) for position in range(steps)]
+            + [("tensor", position) for position in range(tensor_steps)]
+        )
+        wires = Wires(send_sems, recv_sems)
+        streams = [vector_stages(wires, "dp", steps, vector_ref, vector_landing, vector_sums, vector_out)]
+        for which in range(total):
+            pieces = blocks[which].shape[0]
+            for piece in range(pieces):
+                order = far_first if which < 2 and piece == 0 else near_first
+                streams.append(
+                    grad_stages(
+                        wires,
+                        "dp",
+                        order,
+                        sources[which].at[piece],
+                        [landing.at[piece] for landing in landings[which]],
+                        results[which].at[piece],
+                    )
+                )
+        for place, cut in enumerate(cuts):
+            streams.insert(
+                1 + place,
+                share_stages(wires, "tensor", tensor_steps, part_ref, part_landing, part_sums, part_out, cut),
+            )
+        run_wavefront(streams)
+        wires.finish()
+
+    copies = steps + sum(block.shape[0] for block in blocks) * 2 * steps + len(cuts) * (tensor_steps + 1)
+    scratch_shapes = []
+    for block in blocks:
+        for step in range(steps):
+            scratch_shapes.append(
+                pltpu.VMEM((block.shape[0], count >> (step + 1), *block.shape[2:]), jnp.bfloat16)
+            )
+    scratch_shapes += [
+        pltpu.VMEM((steps, *vectors.shape), jnp.float32),
+        pltpu.VMEM((steps, *vectors.shape), jnp.float32),
+        pltpu.VMEM((tensor_steps, rows // 2, width), jnp.bfloat16),
+        pltpu.VMEM((tensor_steps, rows // 2, width), jnp.bfloat16),
+        pltpu.SemaphoreType.DMA((copies,)),
+        pltpu.SemaphoreType.DMA((copies,)),
+    ]
+    outs = pl.pallas_call(
+        kernel,
+        out_shape=[jax.ShapeDtypeStruct(block.shape, jnp.bfloat16) for block in blocks]
+        + [
+            jax.ShapeDtypeStruct(vectors.shape, jnp.float32),
+            jax.ShapeDtypeStruct((2, rows // 2, width), jnp.bfloat16),
+        ],
+        in_specs=[VMEM_SPEC] * (total + 2),
+        out_specs=[VMEM_SPEC] * (total + 2),
+        scratch_shapes=scratch_shapes,
+        compiler_params=pltpu.CompilerParams(collective_id=1, has_side_effects=True),
+        name="grad_sum",
+    )(*blocks, vectors, part.reshape(2, rows // 2, width))
+    summed = [out.reshape(grad.shape).astype(jnp.float32) for out, grad in zip(outs, grads)]
+    return summed, outs[total], outs[total + 1].reshape(rows, width)
 
 
 def per_device(
@@ -61,7 +355,12 @@
     cotangent,
 ):
     f32 = jnp.float32
-    slot_count, length, model_width = images.shape
+    slot_count, true_length, model_width = images.shape
+    length = -(-true_length // ROW_TILE) * ROW_TILE
+    token_pad = ((0, 0), (0, length - true_length), (0, 0))
+    images = jnp.pad(images, token_pad)
+    cotangent = jnp.pad(cotangent, token_pad)
+    key_live = jnp.arange(length) < true_length
     local_width = qkv_weight.shape[2]
     local_heads = local_width // HEAD_DIM
     row_count = slot_count * length
@@ -84,6 +383,7 @@
     scores = (
         jnp.einsum("bqhd,bkhd->bhqk", queries, key_heads, preferred_element_type=f32) * score_scale
     )
+    scores = jnp.where(key_live, scores, -jnp.inf)
     row_peak = jnp.max(scores, axis=-1, keepdims=True)
     log_total = row_peak + jnp.log(jnp.sum(jnp.exp(scores - row_peak), axis=-1, keepdims=True))
     probs_full = jnp.exp(scores - log_total)
@@ -95,7 +395,7 @@
     attn_part = jnp.dot(context_rows, out_weight, preferred_element_type=f32)
     resid_rows = (
         row_values
-        + lax.psum(attn_part.astype(jnp.bfloat16), "tensor").astype(jnp.float32)
+        + tensor_sum(attn_part.astype(jnp.bfloat16)).astype(jnp.float32)
         + out_bias
     )
     norm_two, scaled_two, inverse_two = norm_forward(resid_rows, second_norm_gain, second_norm_bias)
@@ -103,12 +403,6 @@
     pre_act = jnp.dot(norm_two, fc1_weight, preferred_element_type=f32) + fc1_bias
     act_half = to_half(gelu_value(pre_act))
     mlp_part = jnp.dot(act_half, fc2_weight, preferred_element_type=f32)
-    final_rows = (
-        resid_rows
-        + lax.psum(mlp_part.astype(jnp.bfloat16), "tensor").astype(jnp.float32)
-        + fc2_bias
-    )
-    block_out = to_half(final_rows * row_live).reshape(slot_count, length, model_width)
     inv_images = 1.0 / (slot_count * lax.axis_size("dp"))
     grad_final = cotangent.reshape(row_count, model_width).astype(f32) * row_live
     grad_final_half = to_half(grad_final)
@@ -116,15 +410,9 @@
     grad_pre = grad_act * gelu_slope(pre_act)
     grad_pre_half = to_half(grad_pre)
     two_part = jnp.dot(grad_pre_half, fc1_weight.T, preferred_element_type=f32)
-    grad_norm_two = lax.psum(two_part.astype(jnp.bfloat16), "tensor").astype(jnp.float32)
+    grad_norm_two = tensor_sum(two_part.astype(jnp.bfloat16)).astype(jnp.float32)
     back_two, gain_two, shift_two = norm_backward(
         grad_norm_two, scaled_two, inverse_two, second_norm_gain
-    )
-    mlp_grads = (
-        jnp.dot(norm_two.T, grad_pre_half, preferred_element_type=f32) * inv_images,
-        jnp.sum(grad_pre, axis=0, keepdims=True) * inv_images,
-        jnp.dot(act_half.T, grad_final_half, preferred_element_type=f32) * inv_images,
-        jnp.stack([gain_two, shift_two, jnp.sum(grad_final, axis=0)]) * inv_images,
     )
     grad_resid = grad_final + back_two
     grad_resid_half = to_half(grad_resid)
@@ -152,70 +440,54 @@
         row_count, 3 * local_width
     )
     one_part = jnp.dot(grad_qkv_half, qkv_flat.T, preferred_element_type=f32)
-    grad_norm_one = lax.psum(one_part.astype(jnp.bfloat16), "tensor").astype(jnp.float32)
+    grad_norm_one = tensor_sum(one_part.astype(jnp.bfloat16)).astype(jnp.float32)
     back_one, gain_one, shift_one = norm_backward(
         grad_norm_one, scaled_one, inverse_one, first_norm_gain
     )
-    input_grad = to_half(grad_resid + back_one).reshape(slot_count, length, model_width)
-    attn_grads = (
-        jnp.dot(norm_one.T, grad_qkv_half, preferred_element_type=f32) * inv_images,
-        jnp.stack([jnp.sum(grad_queries, axis=0), jnp.sum(grad_values, axis=0)]) * inv_images,
-        jnp.dot(context_rows.T, grad_resid_half, preferred_element_type=f32) * inv_images,
-        jnp.stack([gain_one, shift_one, jnp.sum(grad_resid, axis=0)]) * inv_images,
-    )
-    shares = (
-        lax.psum_scatter(attn_grads[0], "dp", scatter_dimension=1, tiled=True),
-        lax.psum_scatter(attn_grads[1], "dp", scatter_dimension=1, tiled=True),
-        lax.psum_scatter(attn_grads[2], "dp", scatter_dimension=1, tiled=True),
-        lax.psum_scatter(attn_grads[3], "dp", scatter_dimension=1, tiled=True),
-        lax.psum_scatter(mlp_grads[0], "dp", scatter_dimension=1, tiled=True),
-        lax.psum_scatter(mlp_grads[1], "dp", scatter_dimension=1, tiled=True),
-        lax.psum_scatter(mlp_grads[2], "dp", scatter_dimension=1, tiled=True),
-        lax.psum_scatter(mlp_grads[3], "dp", scatter_dimension=1, tiled=True),
-    )
-    gathered = (
-        lax.all_gather(shares[0].astype(jnp.bfloat16), "dp", axis=1, tiled=True).astype(
-            jnp.float32
-        ),
-        lax.all_gather(shares[1].astype(jnp.bfloat16), "dp", axis=1, tiled=True).astype(
-            jnp.float32
-        ),
-        lax.all_gather(shares[2].astype(jnp.bfloat16), "dp", axis=1, tiled=True).astype(
-            jnp.float32
-        ),
-        lax.all_gather(shares[3].astype(jnp.bfloat16), "dp", axis=1, tiled=True).astype(
-            jnp.float32
-        ),
-        lax.all_gather(shares[4].astype(jnp.bfloat16), "dp", axis=1, tiled=True).astype(
-            jnp.float32
-        ),
-        lax.all_gather(shares[5].astype(jnp.bfloat16), "dp", axis=1, tiled=True).astype(
-            jnp.float32
-        ),
-        lax.all_gather(shares[6].astype(jnp.bfloat16), "dp", axis=1, tiled=True).astype(
-            jnp.float32
-        ),
-        lax.all_gather(shares[7].astype(jnp.bfloat16), "dp", axis=1, tiled=True).astype(
-            jnp.float32
-        ),
-    )
-    attn_full = gathered[:4]
-    mlp_full = gathered[4:]
+    input_grad = to_half(grad_resid + back_one).reshape(slot_count, length, model_width)[:, :true_length]
+    weight_grads = [
+        to_half(jnp.dot(left.T, right, preferred_element_type=f32) * inv_images)
+        for left, right in (
+            (norm_two, grad_pre_half),
+            (act_half, grad_final_half),
+            (norm_one, grad_qkv_half),
+            (context_rows, grad_resid_half),
+        )
+    ]
+    rows = [
+        gain_one,
+        shift_one,
+        jnp.sum(grad_resid, axis=0),
+        gain_two,
+        shift_two,
+        jnp.sum(grad_final, axis=0),
+        jnp.sum(grad_pre, axis=0),
+        jnp.sum(grad_queries, axis=0),
+        jnp.sum(grad_values, axis=0),
+    ]
+    vector_width = -(-max(row.shape[0] for row in rows) // 128) * 128
+    vectors = jnp.stack([jnp.pad(row, (0, vector_width - row.shape[0])) for row in rows])
+    vectors = jnp.pad(vectors * inv_images, ((0, -len(rows) % 8), (0, 0)))
+    (fc1_grad, fc2_grad, qkv_grad, out_grad), vectors, mlp_sum = grad_sum(
+        weight_grads, vectors, to_half(mlp_part)
+    )
+    final_rows = resid_rows + mlp_sum.astype(f32) + fc2_bias
+    block_out = to_half(final_rows * row_live).reshape(slot_count, length, model_width)[:, :true_length]
     return (
         block_out,
         input_grad,
-        attn_full[3][0],
-        attn_full[3][1],
-        attn_full[0].reshape(model_width, 3, local_width),
-        attn_full[1],
-        attn_full[2],
-        attn_full[3][2],
-        mlp_full[3][0],
-        mlp_full[3][1],
-        mlp_full[0],
-        mlp_full[1][0],
-        mlp_full[2],
-        mlp_full[3][2],
+        vectors[0, :model_width],
+        vectors[1, :model_width],
+        qkv_grad.reshape(model_width, 3, local_width),
+        vectors[7:9, :local_width],
+        out_grad,
+        vectors[2, :model_width],
+        vectors[3, :model_width],
+        vectors[4, :model_width],
+        fc1_grad,
+        vectors[6, : fc1_bias.shape[0]],
+        fc2_grad,
+        vectors[5, :model_width],
     )
 
 

time: 743 us -> 253 us (0.34)
  waiting for transfers between devices: 455 us -> 0 us
  Pallas kernels: 0 us -> 170 us
  blocking collectives: 158 us -> 0 us
  local copies, waits for them, and re-layouts: 47.1 us -> 29.3 us
  between operations: 16.8 us -> 2.06 us
  matrix products: 41.1 us -> 28.6 us
    pallas_call x0 -> x4, Pallas kernels: none -> 170 us  [the longest x1 117 us: grad_sum(): pl.pallas_call(kernel, out_shape=[jax.ShapeDtypeStruct(block.shape, jnp.b...]
    unnamed x16 -> x0, waiting for transfers between devices: 166 us -> none
    reduce_scatter x3 -> x0, waiting for transfers between devices: 151 us -> none  [the longest x1 61.4 us: per_device(): lax.psum_scatter(mlp_grads[0], 'dp', scatter_dimension=1, tiled=True)]
    all_gather x5 -> x0, blocking collectives: 121 us -> none  [the longest x1 33.5 us: per_device(): lax.all_gather(shares[0].astype(jnp.bfloat16), 'dp', axis=1, tiled=True)]
    psum x3 -> x0, waiting for transfers between devices: 90.5 us -> none  [the longest x1 33.3 us: per_device(): lax.psum(attn_part.astype(jnp.bfloat16), 'tensor').astype(jnp.float32)]
    all_gather x2 -> x0, waiting for transfers between devices: 48.7 us -> none  [the longest x1 39.8 us: per_device(): lax.all_gather(shares[6].astype(jnp.bfloat16), 'dp', axis=1, tiled=True)]
    unnamed x2 -> x0, blocking collectives: 36.6 us -> none
    unnamed x97 -> x83, local copies, waits for them, and re-layouts: 26.6 us -> 9.76 us
  transfers between devices with their start and end apart: 12 -> 0, of which waited for: 12 -> 0; matrix products, arithmetic and copies ran while one was open for 7% -> 0% of each run, Pallas kernels for 0% -> 0%
where the time goes in v1:
time: 253 us; the launch traced here: 252 us
  Pallas kernels  170 us (67%)
  local copies, waits for them, and re-layouts  29.3 us (12%)
  matrix products  28.6 us (11%)
  other arithmetic  21.6 us (9%)
    pallas_call x1, Pallas kernels, grad_sum(): pl.pallas_call(kernel, out_shape=[jax.ShapeDtypeStruct(block.shape, jnp.b...  117 us
    pallas_call x3, Pallas kernels, tensor_sum(): pl.pallas_call(kernel, out_shape=jax.ShapeDtypeStruct((2, rows // 2, widt...  53.6 us
    unnamed x83, local copies, waits for them, and re-layouts  9.76 us
    convert_element_type x7, other arithmetic, to_half(): return array_in.astype(jnp.bfloat16)  6.89 us
    dot_general x4, matrix products, per_device(): jnp.dot(left.T, right, preferred_element_type=f32) * inv_images  6.74 us

profile of v1, /device:TPU:0, one launch (start us, length us, event | category | flops | bytes accessed | tf_op | source)
XLA Modules:
  0.0 251.8 jit_solution(9061440762428020753)
XLA Ops:
  7.8 1.3 fusion.77
  11.7 2.2 convolution_convert_fusion.2
  13.9 18.0 %tensor_sum.3 = bf16[2,208,768]{2,1,0:T(8,128)(2,1)} custom-call(bf16[2,208,768]{2,1,0:T(8,128)(2,1)} %bitcast.117), custom_call_target="tpu_custom_call" | custom-call | tf_op jit(solution)/shard_map/tensor_sum/pallas_call | solution.py:244
  32.0 1.4 fusion.71
  33.5 2.4 multiply_reduce_fusion.3
  36.0 1.6 add_convert_fusion
  37.6 1.6 multiply_convert_fusion.3
  40.2 1.8 multiply_convert_fusion.1
  42.0 1.6 convolution_convert_fusion.1
  43.6 18.3 %tensor_sum.4 = bf16[2,208,768]{2,1,0:T(8,128)(2,1)} custom-call(bf16[2,208,768]{2,1,0:T(8,128)(2,1)} %bitcast.124), custom_call_target="tpu_custom_call" | custom-call | tf_op jit(solution)/shard_map/tensor_sum/pallas_call | solution.py:244
  61.8 2.1 multiply_reduce_fusion.1
  64.1 2.3 fusion.20
  69.6 1.8 copy.64
  71.4 1.8 stack_reshape.14
  73.2 3.3 %multiply_convert_fusion = bf16[768,768]{1,0:T(8,128)(2,1)} fusion(bf16[416,768]{1,0:T(8,128)(2,1)} %get-tuple-element.88, bf16[416,768]{1,0:T(8,128)(2,1)} %fusion.30), kind=kOutput, calls=%fused_computation.1 | convolution fusion | flops 491913216 | bytes 2457600 | tf_op jit(solution)/shard_map/dot_general | solution.py:449
  76.5 1.5 convolution_convert_fusion
  78.0 2.0 fusion.72
  82.1 1.4 fusion.57
  83.6 3.2 %fusion.42 = bf16[2,208,3,64]{1,3,2,0:T(8,128)(2,1)} fusion(f32[2,3,208,208]{2,3,1,0:T(8,128)} %fusion.57, f32[2,3,208,208]{2,3,1,0:T(8,128)S(1)} %get-tuple-element.87, f32[2,3,208]{2,1,0:T(4,128)S(1)} %log_add_fusion, bf16[2,208,3,64]{1,0,3,2:T(2,128)(2,1)} %reshape_squeeze.10), kind=kOutput, calls=%fused_computation.82 | convolution fusion | flops 35125168 | bytes 2401152 | tf_op jit(solution)/shard_map/bhqk,bqhd->bkhd/dot_general | solution.py:433
  86.7 2.4 fusion.75
  92.5 1.3 copy.65
  93.8 2.7 %fusion.7 = bf16[416,768]{1,0:T(8,128)(2,1)} fusion(bf16[416,3,192]{0,2,1:T(8,128)(2,1)S(1)} %copy-done.24, bf16[768,3,192]{0,2,1:T(8,128)(2,1)} %param.19), kind=kOutput, calls=%fused_computation.22 | convolution fusion | flops 368369664 | bytes 2002944 | tf_op jit(solution)/shard_map/dot_general | solution.py:442
  96.5 17.3 %tensor_sum.5 = bf16[2,208,768]{2,1,0:T(8,128)(2,1)} custom-call(bf16[2,208,768]{2,1,0:T(8,128)(2,1)} %bitcast.125), custom_call_target="tpu_custom_call" | custom-call | tf_op jit(solution)/shard_map/tensor_sum/pallas_call | solution.py:244
  113.8 1.9 multiply_reduce_fusion
  118.1 116.7 %grad_sum.1 = (bf16[3,8,32,768]{3,2,1,0:T(8,128)(2,1)}, bf16[3,8,32,768]{3,2,1,0:T(8,128)(2,1)}, bf16[3,8,32,576]{3,2,1,0:T(8,128)(2,1)}, bf16[1,8,24,768]{3,2,1...) custom-call(bf16[3,8,32,768]{3,2,1,0:T(8,128)(2,1)} %bitcast.120, bf16[3,8,32,768]{3,2,1,0:T(8,128)(2,1)} %bitcast.121, ...), custom_call_target="tpu_custom_call" | custom-call | tf_op jit(solution)/shard_map/grad_sum/pallas_call | solution.py:323
  234.8 1.4 fusion.28
  237.4 1.3 slice.54
  238.7 1.7 slice_reduce_fusion
  241.3 1.7 bitcast_convert_fusion.1
  243.0 1.7 bitcast_convert_fusion
  244.6 3.0 %reshape.508 = f32[768,3,192]{2,1,0:T(4,128)} reshape(bf16[3,8,32,576]{3,2,1,0:T(8,128)(2,1)S(1)} %copy-done.13) | data formatting | bytes 2654208 | tf_op jit(solution)/shard_map/convert_element_type | solution.py:336
  247.6 4.2 %copy.68 = f32[768,3,192]{0,2,1:T(8,128)} copy(f32[768,3,192]{2,1,0:T(4,128)} %reshape.508) | data formatting | bytes 3538944
  (144 shorter events, 23.2 us)
Async XLA Ops:
  0.6 37.0 %copy-start = (bf16[768,768]{1,0:T(8,128)(2,1)S(1)}, bf16[768,768]{1,0:T(8,128)(2,1)}, u32[]{:S(2)}) copy-start(bf16[768,768]{1,0:T(8,128)(2,1)} %param.25) | copy-start | bytes 3538948
  0.7 3.5 %copy-start.20 = (bf16[2,197,768]{2,0,1:T(2,128)(2,1)S(1)}, bf16[2,197,768]{2,0,1:T(2,128)(2,1)}, u32[]{:S(2)}) copy-start(bf16[2,197,768]{2,0,1:T(2,128)(2,1)} %param.29) | copy-start | bytes 1815556
  1.5 76.5 %copy-start.28 = (f32[2]{0:T(128)}, f32[2]{0:T(128)S(1)}, u32[]{:S(2)}) copy-start(f32[2]{0:T(128)S(1)} %compare_convert_fusion) | copy-start | bytes 28
  4.3 2.3 copy-start.5
  4.3 1.6 copy-start.35
  7.6 1.7 copy-start.14
  11.7 21.7 %copy-start.8 = (bf16[416,192]{0,1:T(8,128)(2,1)}, bf16[416,192]{0,1:T(8,128)(2,1)S(1)}, u32[]{:S(2)}) copy-start(bf16[416,192]{0,1:T(8,128)(2,1)S(1)} %reshape.496) | copy-start | bytes 479236
  11.7 20.3 %copy-start.22 = (f32[768]{0:T(1024)S(1)}, f32[768]{0:T(1024)}, u32[]{:S(2)}) copy-start(f32[768]{0:T(1024)} %param.22) | copy-start | bytes 9220
  33.4 2.6 %copy-start.25 = (f32[768]{0:T(1024)S(1)}, f32[768]{0:T(1024)}, u32[]{:S(2)}) copy-start(f32[768]{0:T(1024)} %param.23) | copy-start | bytes 9220
  33.4 2.6 %copy-start.31 = (f32[768]{0:T(1024)S(1)}, f32[768]{0:T(1024)}, u32[]{:S(2)}) copy-start(f32[768]{0:T(1024)} %param.24) | copy-start | bytes 9220
  35.9 1.7 copy-start.36
  37.6 1.6 copy-start.19
  37.6 1.6 copy-start.33
  64.1 2.3 copy-start.12
  73.2 3.3 %copy-start.34 = (bf16[768,768]{1,0:T(8,128)(2,1)S(1)}, bf16[768,768]{1,0:T(8,128)(2,1)}, u32[]{:S(2)}) copy-start(bf16[768,768]{1,0:T(8,128)(2,1)} %param.27) | copy-start | bytes 3538948
  73.2 3.3 %copy-start.37 = (bf16[416,768]{1,0:T(8,128)(2,1)S(1)}, bf16[416,768]{1,0:T(8,128)(2,1)}, u32[]{:S(2)}) copy-start(bf16[416,768]{1,0:T(8,128)(2,1)} %get-tuple-element.88) | copy-start | bytes 1916932
  76.5 1.5 copy-start.1
  76.5 1.5 copy-start.4
  76.5 1.5 copy-start.6
  80.0 2.2 copy-start.2
  83.6 3.2 %copy-start.15 = (bf16[2,208,3,64]{1,0,3,2:T(2,128)(2,1)S(1)}, bf16[2,208,3,64]{1,0,3,2:T(2,128)(2,1)}, u32[]{:S(2)}) copy-start(bf16[2,208,3,64]{1,0,3,2:T(2,128)(2,1)} %copy-done.14) | copy-start | bytes 479236
  89.2 1.8 copy-start.16
  90.4 1.4 copy-start.18
  113.8 1.9 copy-start.3
  115.7 1.6 copy-start.27
  118.1 116.7 %copy-start.7 = (f32[2,208,768]{2,1,0:T(8,128)S(1)}, f32[2,208,768]{2,1,0:T(8,128)}, u32[]{:S(2)}) copy-start(f32[2,208,768]{2,1,0:T(8,128)} %get-tuple-element.71) | copy-start | bytes 3833860
  118.1 116.7 %copy-start.29 = (f32[2]{0:T(128)S(1)}, f32[2]{0:T(128)}, u32[]{:S(2)}) copy-start(f32[2]{0:T(128)} %copy-done.28) | copy-start | bytes 28
  118.1 116.7 %copy-start.32 = (f32[768]{0:T(1024)S(1)}, f32[768]{0:T(1024)}, u32[]{:S(2)}) copy-start(f32[768]{0:T(1024)} %param.28) | copy-start | bytes 9220
  234.8 5.6 %copy-start.21 = (bf16[1,8,24,768]{3,2,1,0:T(8,128)(2,1)S(1)}, bf16[1,8,24,768]{3,2,1,0:T(8,128)(2,1)}, u32[]{:S(2)}) copy-start(bf16[1,8,24,768]{3,2,1,0:T(8,128)(2,1)} %get-tuple-element.23) | copy-start | bytes 884740
  236.2 5.1 %copy-start.11 = (bf16[3,8,32,768]{3,2,1,0:T(8,128)(2,1)S(1)}, bf16[3,8,32,768]{3,2,1,0:T(8,128)(2,1)}, u32[]{:S(2)}) copy-start(bf16[3,8,32,768]{3,2,1,0:T(8,128)(2,1)} %get-tuple-element.24) | copy-start | bytes 3538948
  241.3 1.7 copy-start.10
  243.0 1.7 copy-start.13
  (6 other events, 6.5 us)

commit v2 on v1

--- a/solution.py
+++ b/solution.py
@@ -257,84 +257,254 @@
     )(part.reshape(2, rows // 2, width)).reshape(rows, width)
 
 
-def grad_sum(grads, vectors, part):
+def dot_nt(left, right):
+    return lax.dot_general(left, right, (((1,), (1,)), ((), ())), preferred_element_type=jnp.float32)
+
+
+def dot_tn(left, right):
+    return lax.dot_general(left, right, (((0,), (0,)), ((), ())), preferred_element_type=jnp.float32)
+
+
+def dot_nn(left, right):
+    return jnp.dot(left, right, preferred_element_type=jnp.float32)
+
+
+def backward_tail(
+    fc1_grad,
+    fc2_grad,
+    mlp_part,
+    two_part,
+    scaled_two,
+    inverse_two,
+    second_gain,
+    grad_final_half,
+    out_weight,
+    queries_t,
+    keys_t,
+    value_heads,
+    probs,
+    norm_one,
+    context_t,
+    qkv_weight_t,
+    scaled_one,
+    inverse_one,
+    first_gain,
+    vectors,
+):
+    f32 = jnp.float32
     count = lax.axis_size("dp")
     steps = log2_of(count)
     tensor_steps = log2_of(lax.axis_size("tensor"))
-    rows, width = part.shape
+    slots, length, width = two_part.shape
+    local_width = out_weight.shape[0]
+    heads = local_width // HEAD_DIM
     cuts = column_cuts(width, 3)
-    blocks = []
-    for grad in grads:
+    inv_images = 1.0 / (slots * count)
+    score_scale = HEAD_DIM ** (-0.5)
+    share_rows = local_width // count
+    early = []
+    for grad in (fc1_grad, fc2_grad):
         pieces = 3 if grad.shape[0] % (3 * count * ROW_TILE) == 0 else 1
-        blocks.append(grad.reshape(pieces, count, grad.shape[0] // (pieces * count), grad.shape[1]))
-    total = len(blocks)
+        early.append(grad.reshape(pieces, count, grad.shape[0] // (pieces * count), grad.shape[1]))
+    late_shape = (4, count, share_rows, width)
     far_first = [*range(1, steps), 0]
     near_first = [*range(steps)]
 
-    def kernel(*refs):
-        sources, (vector_ref, part_ref) = refs[:total], refs[total : total + 2]
-        results, (vector_out, part_out) = refs[total + 2 : 2 * total + 2], refs[2 * total + 2 : 2 * total + 4]
-        scratch = refs[2 * total + 4 :]
-        landings = [scratch[i * steps : (i + 1) * steps] for i in range(total)]
-        vector_landing, vector_sums, part_landing, part_sums, send_sems, recv_sems = scratch[total * steps :]
+    def kernel(
+        fc1_ref, fc2_ref, mlp_ref, two_ref, scaled_two_ref, inverse_two_ref, second_gain_ref,
+        final_ref, out_weight_ref, queries_ref, keys_ref, values_ref, probs_ref, norm_ref,
+        context_ref, qkv_weight_ref, scaled_one_ref, inverse_one_ref, first_gain_ref, vector_in_ref,
+        fc1_out, fc2_out, late_out, vector_out, mlp_out, input_out,
+        two_sum, one_ref, one_sum, resid, resid_half, late, vector_ref, qkv_t,
+        vector_landing, vector_sums, share_landing, share_sums, send_sems, recv_sems, *landings,
+    ):
         greet(
-            [("dp", position) for position in range(steps)]
-            + [("tensor", position) for position in range(tensor_steps)]
+            [("tensor", position) for position in range(tensor_steps)]
+            + [("dp", position) for position in range(steps)]
         )
         wires = Wires(send_sems, recv_sems)
-        streams = [vector_stages(wires, "dp", steps, vector_ref, vector_landing, vector_sums, vector_out)]
-        for which in range(total):
-            pieces = blocks[which].shape[0]
-            for piece in range(pieces):
-                order = far_first if which < 2 and piece == 0 else near_first
-                streams.append(
-                    grad_stages(
-                        wires,
-                        "dp",
-                        order,
-                        sources[which].at[piece],
-                        [landing.at[piece] for landing in landings[which]],
-                        results[which].at[piece],
-                    )
+        agenda = []
+
+        def plan(time, action):
+            agenda.append((time, len(agenda), action))
+
+        def plan_all(actions, begin, gap, first=None):
+            for place, action in enumerate(actions):
+                plan(begin + gap * place if place or first is None else first, action)
+
+        def shares(which, source, result, begin):
+            for place, cut in enumerate(cuts):
+                stages = share_stages(
+                    wires, "tensor", tensor_steps, source,
+                    share_landing.at[which], share_sums.at[which], result, cut,
                 )
-        for place, cut in enumerate(cuts):
-            streams.insert(
-                1 + place,
-                share_stages(wires, "tensor", tensor_steps, part_ref, part_landing, part_sums, part_out, cut),
+                plan(begin, stages[0])
+                for stage, action in enumerate(stages[1:]):
+                    plan(begin + 2 + 3.5 * stage + 3 * place, action)
+
+        vector_ref[...] = vector_in_ref[...]
+
+        def resid_stage(slot):
+            def stage():
+                grad = two_sum[slot].astype(f32)
+                scaled = scaled_two_ref[slot]
+                back, gain, shift = norm_backward(grad, scaled, inverse_two_ref[slot], second_gain_ref[...])
+                total = final_ref[slot].astype(f32) + back
+                resid[slot] = total
+                resid_half[slot] = to_half(total)
+                for row, value in ((2, jnp.sum(total, axis=0)), (3, gain), (4, shift)):
+                    vector_ref[row : row + 1, :width] += value[None] * inv_images
+
+            return stage
+
+        def head_stage(slot, head):
+            def stage():
+                at = slot * heads + head
+                weight = out_weight_ref[head * HEAD_DIM : (head + 1) * HEAD_DIM]
+                grad_context = to_half(dot_nt(resid_half[slot], weight))
+                grad_context_t = to_half(dot_nt(weight, resid_half[slot]))
+                grad_probs = dot_nt(grad_context, values_ref[at])
+                full = probs_ref[at]
+                inner = jnp.sum(full * grad_probs, axis=-1, keepdims=True)
+                grad_scores = to_half(full * (grad_probs - inner) * score_scale)
+                terms = (
+                    dot_nt(keys_ref[at], grad_scores),
+                    dot_nn(queries_ref[at], grad_scores),
+                    dot_nn(grad_context_t, to_half(full)),
+                )
+                ones = jnp.ones((8, length), f32)
+                for part, term in enumerate(terms):
+                    begin = part * local_width + head * HEAD_DIM
+                    qkv_t[slot, begin : begin + HEAD_DIM, :] = to_half(term)
+                    if part != 1:
+                        sums = lax.dot_general(
+                            ones, term, (((1,), (1,)), ((), ())),
+                            precision=lax.Precision.HIGHEST, preferred_element_type=f32,
+                        )
+                        row = 7 + (part // 2) * heads + head
+                        vector_ref[row : row + 1, :HEAD_DIM] += sums[0:1] * inv_images
+
+            return stage
+
+        def late_stage(part):
+            def stage():
+                total = jnp.zeros((local_width, width), f32)
+                for slot in range(slots):
+                    if part < 3:
+                        left = qkv_t[slot, part * local_width : (part + 1) * local_width, :]
+                        total += dot_nn(left, norm_ref[slot])
+                    else:
+                        total += dot_nn(context_ref[slot], resid_half[slot])
+                total = total * inv_images
+                for block in range(count):
+                    late[part, block] = to_half(total[block * share_rows : (block + 1) * share_rows])
+
+            return stage
+
+        def one_stage(slot):
+            def stage():
+                one_ref[slot] = to_half(dot_tn(qkv_t[slot], qkv_weight_ref[...]))
+
+            return stage
+
+        def input_stage(slot):
+            def stage():
+                grad = one_sum[slot].astype(f32)
+                back, gain, shift = norm_backward(
+                    grad, scaled_one_ref[slot], inverse_one_ref[slot], first_gain_ref[...]
+                )
+                input_out[slot] = to_half(resid[slot] + back)
+                for row, value in ((0, gain), (1, shift)):
+                    vector_ref[row : row + 1, :width] += value[None] * inv_images
+
+            return stage
+
+        shares(0, two_ref, two_sum, -2)
+        streams = 0
+        for which, (source, result) in enumerate(((fc1_ref, fc1_out), (fc2_ref, fc2_out))):
+            for piece in range(early[which].shape[0]):
+                stages = grad_stages(
+                    wires, "dp", far_first if piece == 0 else near_first, source.at[piece],
+                    [landings[which * steps + step].at[piece] for step in range(steps)], result.at[piece],
+                )
+                plan_all(stages, 4 + 6 * streams, 7, 0.5)
+                streams += 1
+        for slot in range(slots):
+            plan(14, resid_stage(slot))
+        for slot in range(slots):
+            for head in range(heads):
+                plan(15 + 1.5 * (slot * heads + head), head_stage(slot, head))
+        for slot in range(slots):
+            plan(25, one_stage(slot))
+        shares(1, one_ref, one_sum, 26)
+        for part in range(4):
+            plan(27 + part, late_stage(part))
+            stages = grad_stages(
+                wires, "dp", near_first, late.at[part],
+                [landings[2 * steps + step].at[part] for step in range(steps)], late_out.at[part],
             )
-        run_wavefront(streams)
+            plan_all(stages, max(4 + 6 * streams, 24 + part), 7, 27 + part)
+            streams += 1
+        for slot in range(slots):
+            plan(42, input_stage(slot))
+        plan_all(
+            vector_stages(wires, "dp", steps, vector_ref, vector_landing, vector_sums, vector_out), 43, 16
+        )
+        shares(2, mlp_ref, mlp_out, 44)
+        for _, _, action in sorted(agenda, key=lambda entry: entry[:2]):
+            action()
         wires.finish()
 
-    copies = steps + sum(block.shape[0] for block in blocks) * 2 * steps + len(cuts) * (tensor_steps + 1)
-    scratch_shapes = []
-    for block in blocks:
-        for step in range(steps):
-            scratch_shapes.append(
-                pltpu.VMEM((block.shape[0], count >> (step + 1), *block.shape[2:]), jnp.bfloat16)
-            )
-    scratch_shapes += [
-        pltpu.VMEM((steps, *vectors.shape), jnp.float32),
-        pltpu.VMEM((steps, *vectors.shape), jnp.float32),
-        pltpu.VMEM((tensor_steps, rows // 2, width), jnp.bfloat16),
-        pltpu.VMEM((tensor_steps, rows // 2, width), jnp.bfloat16),
+    copies = steps + (sum(block.shape[0] for block in early) + 4) * 2 * steps + 3 * len(cuts) * (tensor_steps + 1)
+    scratch_shapes = [
+        pltpu.VMEM(two_part.shape, jnp.bfloat16),
+        pltpu.VMEM(two_part.shape, jnp.bfloat16),
+        pltpu.VMEM(two_part.shape, jnp.bfloat16),
+        pltpu.VMEM(two_part.shape, f32),
+        pltpu.VMEM(two_part.shape, jnp.bfloat16),
+        pltpu.VMEM(late_shape, jnp.bfloat16),
+        pltpu.VMEM(vectors.shape, f32),
+        pltpu.VMEM((slots, 3 * local_width, length), jnp.bfloat16),
+        pltpu.VMEM((steps, *vectors.shape), f32),
+        pltpu.VMEM((steps, *vectors.shape), f32),
+        pltpu.VMEM((3, tensor_steps, length, width), jnp.bfloat16),
+        pltpu.VMEM((3, tensor_steps, length, width), jnp.bfloat16),
         pltpu.SemaphoreType.DMA((copies,)),
         pltpu.SemaphoreType.DMA((copies,)),
     ]
-    outs = pl.pallas_call(
+    for shape in (early[0].shape, early[1].shape, late_shape):
+        for step in range(steps):
+            scratch_shapes.append(pltpu.VMEM((shape[0], count >> (step + 1), *shape[2:]), jnp.bfloat16))
+    fc1_sum, fc2_sum, late_sum, vectors, mlp_sum, input_grad = pl.pallas_call(
         kernel,
-        out_shape=[jax.ShapeDtypeStruct(block.shape, jnp.bfloat16) for block in blocks]
-        + [
-            jax.ShapeDtypeStruct(vectors.shape, jnp.float32),
-            jax.ShapeDtypeStruct((2, rows // 2, width), jnp.bfloat16),
+        out_shape=[
+            jax.ShapeDtypeStruct(early[0].shape, jnp.bfloat16),
+            jax.ShapeDtypeStruct(early[1].shape, jnp.bfloat16),
+            jax.ShapeDtypeStruct(late_shape, jnp.bfloat16),
+            jax.ShapeDtypeStruct(vectors.shape, f32),
+            jax.ShapeDtypeStruct(mlp_part.shape, jnp.bfloat16),
+            jax.ShapeDtypeStruct(two_part.shape, jnp.bfloat16),
         ],
-        in_specs=[VMEM_SPEC] * (total + 2),
-        out_specs=[VMEM_SPEC] * (total + 2),
+        in_specs=[VMEM_SPEC] * 20,
+        out_specs=[VMEM_SPEC] * 6,
         scratch_shapes=scratch_shapes,
         compiler_params=pltpu.CompilerParams(collective_id=1, has_side_effects=True),
-        name="grad_sum",
-    )(*blocks, vectors, part.reshape(2, rows // 2, width))
-    summed = [out.reshape(grad.shape).astype(jnp.float32) for out, grad in zip(outs, grads)]
-    return summed, outs[total], outs[total + 1].reshape(rows, width)
+        name="backward_tail",
+    )(
+        *early, mlp_part, two_part, scaled_two, inverse_two, second_gain, grad_final_half, out_weight,
+        queries_t, keys_t, value_heads, probs, norm_one, context_t, qkv_weight_t, scaled_one,
+        inverse_one, first_gain, vectors,
+    )
+    late_sum = late_sum.reshape(4, local_width, width)
+    return (
+        fc1_sum.reshape(fc1_grad.shape).astype(f32),
+        fc2_sum.reshape(fc2_grad.shape).astype(f32),
+        jnp.transpose(late_sum[:3], (2, 0, 1)).astype(f32),
+        late_sum[3].astype(f32),
+        vectors,
+        mlp_sum,
+        input_grad,
+    )
 
 
 def per_device(
@@ -392,6 +562,7 @@
         jnp.einsum("bhqk,bkhd->bqhd", probs_half, value_heads, preferred_element_type=f32)
     )
     context_rows = context.reshape(row_count, local_width)
+    context_t = jnp.transpose(context, (0, 2, 3, 1)).reshape(slot_count, local_width, length)
     attn_part = jnp.dot(context_rows, out_weight, preferred_element_type=f32)
     resid_rows = (
         row_values
@@ -410,76 +581,48 @@
     grad_pre = grad_act * gelu_slope(pre_act)
     grad_pre_half = to_half(grad_pre)
     two_part = jnp.dot(grad_pre_half, fc1_weight.T, preferred_element_type=f32)
-    grad_norm_two = tensor_sum(two_part.astype(jnp.bfloat16)).astype(jnp.float32)
-    back_two, gain_two, shift_two = norm_backward(
-        grad_norm_two, scaled_two, inverse_two, second_norm_gain
-    )
-    grad_resid = grad_final + back_two
-    grad_resid_half = to_half(grad_resid)
-    grad_context = to_half(
-        jnp.dot(grad_resid_half, out_weight.T, preferred_element_type=f32)
-    ).reshape(head_shape)
-    grad_probs = jnp.einsum(
-        "bqhd,bkhd->bhqk", grad_context, value_heads, preferred_element_type=f32
-    )
-    grad_scores = to_half(
-        probs_full
-        * (grad_probs - jnp.sum(probs_full * grad_probs, axis=-1, keepdims=True))
-        * score_scale
-    )
-    grad_queries = jnp.einsum(
-        "bhqk,bkhd->bqhd", grad_scores, key_heads, preferred_element_type=f32
-    ).reshape(row_count, local_width)
-    grad_keys = jnp.einsum(
-        "bhqk,bqhd->bkhd", grad_scores, queries, preferred_element_type=f32
-    ).reshape(row_count, local_width)
-    grad_values = jnp.einsum(
-        "bhqk,bqhd->bkhd", probs_half, grad_context, preferred_element_type=f32
-    ).reshape(row_count, local_width)
-    grad_qkv_half = to_half(jnp.stack([grad_queries, grad_keys, grad_values], axis=1)).reshape(
-        row_count, 3 * local_width
-    )
-    one_part = jnp.dot(grad_qkv_half, qkv_flat.T, preferred_element_type=f32)
-    grad_norm_one = tensor_sum(one_part.astype(jnp.bfloat16)).astype(jnp.float32)
-    back_one, gain_one, shift_one = norm_backward(
-        grad_norm_one, scaled_one, inverse_one, first_norm_gain
-    )
-    input_grad = to_half(grad_resid + back_one).reshape(slot_count, length, model_width)[:, :true_length]
-    weight_grads = [
-        to_half(jnp.dot(left.T, right, preferred_element_type=f32) * inv_images)
-        for left, right in (
-            (norm_two, grad_pre_half),
-            (act_half, grad_final_half),
-            (norm_one, grad_qkv_half),
-            (context_rows, grad_resid_half),
-        )
-    ]
-    rows = [
-        gain_one,
-        shift_one,
-        jnp.sum(grad_resid, axis=0),
-        gain_two,
-        shift_two,
-        jnp.sum(grad_final, axis=0),
-        jnp.sum(grad_pre, axis=0),
-        jnp.sum(grad_queries, axis=0),
-        jnp.sum(grad_values, axis=0),
-    ]
-    vector_width = -(-max(row.shape[0] for row in rows) // 128) * 128
+    per_slot = (slot_count, length, model_width)
+    per_head = slot_count * local_heads
+    rows = [jnp.sum(grad_final, axis=0) * inv_images, jnp.sum(grad_pre, axis=0) * inv_images]
+    vector_width = -(-max(model_width, fc1_bias.shape[0]) // 128) * 128
+    vector_rows = -(-(7 + 2 * local_heads) // 8) * 8
     vectors = jnp.stack([jnp.pad(row, (0, vector_width - row.shape[0])) for row in rows])
-    vectors = jnp.pad(vectors * inv_images, ((0, -len(rows) % 8), (0, 0)))
-    (fc1_grad, fc2_grad, qkv_grad, out_grad), vectors, mlp_sum = grad_sum(
-        weight_grads, vectors, to_half(mlp_part)
-    )
-    final_rows = resid_rows + mlp_sum.astype(f32) + fc2_bias
-    block_out = to_half(final_rows * row_live).reshape(slot_count, length, model_width)[:, :true_length]
+    vectors = jnp.pad(vectors, ((5, vector_rows - 7), (0, 0)))
+    fc1_grad = to_half(jnp.dot(norm_two.T, grad_pre_half, preferred_element_type=f32) * inv_images)
+    fc2_grad = to_half(jnp.dot(act_half.T, grad_final_half, preferred_element_type=f32) * inv_images)
+    fc1_grad, fc2_grad, qkv_grad, out_grad, vectors, mlp_sum, input_grad = backward_tail(
+        fc1_grad,
+        fc2_grad,
+        to_half(mlp_part).reshape(per_slot),
+        to_half(two_part).reshape(per_slot),
+        scaled_two.reshape(per_slot),
+        inverse_two.reshape(slot_count, length, 1),
+        second_norm_gain[None],
+        grad_final_half.reshape(per_slot),
+        out_weight,
+        jnp.transpose(queries, (0, 2, 3, 1)).reshape(per_head, HEAD_DIM, length),
+        jnp.transpose(key_heads, (0, 2, 3, 1)).reshape(per_head, HEAD_DIM, length),
+        jnp.transpose(value_heads, (0, 2, 1, 3)).reshape(per_head, length, HEAD_DIM),
+        probs_full.reshape(per_head, length, length),
+        norm_one.reshape(per_slot),
+        context_t,
+        qkv_flat.T,
+        scaled_one.reshape(per_slot),
+        inverse_one.reshape(slot_count, length, 1),
+        first_norm_gain[None],
+        vectors,
+    )
+    final_rows = resid_rows + mlp_sum.reshape(row_count, model_width).astype(f32) + fc2_bias
+    block_out = to_half(final_rows * row_live).reshape(per_slot)[:, :true_length]
+    input_grad = input_grad[:, :true_length]
+    qv_grad = vectors[7 : 7 + 2 * local_heads, :HEAD_DIM].reshape(2, local_width)
     return (
         block_out,
         input_grad,
         vectors[0, :model_width],
         vectors[1, :model_width],
-        qkv_grad.reshape(model_width, 3, local_width),
-        vectors[7:9, :local_width],
+        qkv_grad,
+        qv_grad,
         out_grad,
         vectors[2, :model_width],
         vectors[3, :model_width],

time: 253 us -> 173 us (0.68)
  Pallas kernels: 170 us -> 126 us
  matrix products: 28.6 us -> 12.7 us
  local copies, waits for them, and re-layouts: 29.3 us -> 17.1 us
  other arithmetic: 21.6 us -> 15.2 us
    pallas_call x3 -> x1, Pallas kernels: 53.6 us -> 18 us  [tensor_sum(): pl.pallas_call(kernel, out_shape=jax.ShapeDtypeStruct((2, rows // 2, widt...]
    dot_general x10 -> x2, matrix products: 18.5 us -> 3.7 us  [the longest x1 1.85 us: per_device(): jnp.dot(norm_two.T, grad_pre_half, preferred_element_type=f32) * inv_images]
    pallas_call x1, Pallas kernels: 117 us -> 108 us  [backward_tail(): pl.pallas_call(kernel, out_shape=[jax.ShapeDtypeStruct(early[0].shape, jn...]
    reduce_sum x3 -> x1, other arithmetic: 5.92 us -> 1.05 us  [per_device(): jnp.sum(grad_final, axis=0) * inv_images]
    another operation x16 -> x0, local copies, waits for them, and re-layouts: 4.74 us -> none  [the longest x4 2.05 us: per_device(): jnp.stack([grad_queries, grad_keys, grad_values], axis=1)]
    convert_element_type x7 -> x3, other arithmetic: 6.89 us -> 2.61 us  [to_half(): return array_in.astype(jnp.bfloat16)]
    unnamed x83 -> x48, local copies, waits for them, and re-layouts: 9.76 us -> 6.3 us
    mul x1 -> x4, other arithmetic: 0.01 us -> 3.11 us  [the longest x2 3.1 us: norm_forward(): scaled = centre * inverse]
where the time goes in v2:
time: 173 us; the launch traced here: 172 us
  Pallas kernels  126 us (73%)
  local copies, waits for them, and re-layouts  17.1 us (10%)
  other arithmetic  15.2 us (9%)
  matrix products  12.7 us (7%)
    pallas_call x1, Pallas kernels, backward_tail(): pl.pallas_call(kernel, out_shape=[jax.ShapeDtypeStruct(early[0].shape, jn...  108 us
    pallas_call x1, Pallas kernels, tensor_sum(): pl.pallas_call(kernel, out_shape=jax.ShapeDtypeStruct((2, rows // 2, widt...  18 us
    unnamed x48, local copies, waits for them, and re-layouts  6.3 us

profile of v2, /device:TPU:0, one launch (start us, length us, event | category | flops | bytes accessed | tf_op | source)
XLA Modules:
  0.0 172.5 jit_solution(542809974389615170)
XLA Ops:
  1.7 0.8 fusion.29
  2.5 1.3 broadcast_in_dim.18.first_gain_ref
  3.8 1.3 broadcast_in_dim.17.second_gain_ref
  5.0 1.2 copy.56
  6.7 0.8 copy.68.inverse_one_ref
  7.7 1.0 fusion.9
  8.7 1.0 multiply_reduce_fusion.1
  9.8 1.3 fusion
  12.4 0.7 copy.58
  13.1 0.7 copy.57
  15.0 1.0 convolution_convert_fusion.3
  16.0 1.5 copy.66
  17.8 2.2 %convolution_convert_fusion.2 = bf16[416,768]{1,0:T(8,128)(2,1)} fusion(bf16[416,192]{0,1:T(8,128)(2,1)S(1)} %reshape.331, bf16[192,768]{1,0:T(8,128)(2,1)} %out_weight_ref.1), kind=kOutput, calls=%fused_computation.16 | convolution fusion | flops 123002880 | bytes 1093632 | tf_op jit(solution)/shard_map/dot_general | solution.py:566
  20.0 18.0 %tensor_sum.1 = bf16[2,208,768]{2,1,0:T(8,128)(2,1)} custom-call(bf16[2,208,768]{2,1,0:T(8,128)(2,1)} %bitcast.91), custom_call_target="tpu_custom_call" | custom-call | tf_op jit(solution)/shard_map/tensor_sum/pallas_call | solution.py:244
  38.0 1.4 fusion.27
  40.1 0.8 copy.67.inverse_two_ref
  40.9 1.8 %subtract_multiply_fusion = (f32[2,208,768]{2,1,0:T(8,128)}, f32[2,208,768]{2,1,0:T(8,128)}, f32[2,208,768]{2,1,0:T(8,128)S(1)}) fusion(f32[2,208]{1,0:T(2,128)S(1)} %get-tuple-element.88, f32[2,208]{1,0:T(2,128)S(1)} %broadcast_multiply_fusion.2, f32[768]{0:T(1024)S(1)} %copy-done.13, bf16[2,208,768]{2,1,0:T(8,128)(2,1)S(1)} %copy-done.1, ...), kind=kLoop, calls=%fused_computation.43 | loop fusion | flops 1916928 | bytes 5084416 | tf_op jit(solution)/shard_map/mul | solution.py:23
  43.4 0.7 multiply_convert_fusion.2
  44.8 0.9 fusion.31
  46.4 1.9 %multiply_convert_fusion.1 = bf16[768,768]{1,0:T(8,128)(2,1)} fusion(bf16[416,768]{1,0:T(8,128)(2,1)S(1)} %fusion.14, bf16[416,768]{1,0:T(8,128)(2,1)S(1)} %get-tuple-element.96), kind=kOutput, calls=%fused_computation.1 | convolution fusion | flops 491913216 | bytes 2457600 | tf_op jit(solution)/shard_map/dot_general | solution.py:591
  48.2 1.6 convolution_convert_fusion
  49.8 1.8 %multiply_convert_fusion = bf16[768,768]{1,0:T(8,128)(2,1)} fusion(bf16[416,768]{1,0:T(8,128)(2,1)S(1)} %get-tuple-element.93, bf16[416,768]{1,0:T(8,128)(2,1)S(1)} %copy-done.10), kind=kOutput, calls=%fused_computation | convolution fusion | flops 491913216 | bytes 2457600 | tf_op jit(solution)/shard_map/dot_general | solution.py:592
  51.6 1.6 convolution_convert_fusion.1
  53.2 107.8 %backward_tail.1 = (bf16[3,8,32,768]{3,2,1,0:T(8,128)(2,1)}, bf16[3,8,32,768]{3,2,1,0:T(8,128)(2,1)}, bf16[4,8,24,768]{3,2,1,0:T(8,128)(2,1)}, f32[16,768]{1,0:T...) custom-call(bf16[3,8,32,768]{3,2,1,0:T(8,128)(2,1)} %bitcast.94, bf16[3,8,32,768]{3,2,1,0:T(8,128)(2,1)} %bitcast.95, ...), custom_call_target="tpu_custom_call" | custom-call | tf_op jit(solution)/shard_map/backward_tail/pallas_call | solution.py:478
  161.1 1.3 fusion.17
  162.4 1.3 copy.69
  163.7 0.7 slice_reduce_fusion
  165.1 0.9 bitcast_convert_fusion.2
  166.2 1.3 copy.70
  167.5 1.4 convert_bitcast_fusion
  169.1 0.7 copy-done.7
  169.8 2.7 %bitcast_convert_fusion = (f32[768,768]{1,0:T(8,128)}, f32[768,768]{1,0:T(8,128)}) fusion(bf16[3,8,32,768]{3,2,1,0:T(8,128)(2,1)S(1)} %copy-done.7, bf16[3,8,32,768]{3,2,1,0:T(8,128)(2,1)S(1)} %copy-done.6), kind=kLoop, calls=%fused_computation.44 | loop fusion | flops 1179648 | bytes 7077888 | tf_op jit(solution)/shard_map/convert_element_type | solution.py:501
  (82 shorter events, 7.5 us)
Async XLA Ops:
  0.6 42.3 %copy-start = (bf16[768,768]{1,0:T(8,128)(2,1)S(1)}, bf16[768,768]{1,0:T(8,128)(2,1)}, u32[]{:S(2)}) copy-start(bf16[768,768]{1,0:T(8,128)(2,1)} %param.25) | copy-start | bytes 3538948
  5.0 2.5 %copy-start.11 = (bf16[2,197,768]{2,0,1:T(2,128)(2,1)S(1)}, bf16[2,197,768]{2,0,1:T(2,128)(2,1)}, u32[]{:S(2)}) copy-start(bf16[2,197,768]{2,0,1:T(2,128)(2,1)} %param.29) | copy-start | bytes 1815556
  7.6 2.1 %copy-start.14 = (f32[768]{0:T(1024)S(1)}, f32[768]{0:T(1024)}, u32[]{:S(2)}) copy-start(f32[768]{0:T(1024)} %param.17) | copy-start | bytes 9220
  7.6 2.1 %copy-start.17 = (f32[768]{0:T(1024)S(1)}, f32[768]{0:T(1024)}, u32[]{:S(2)}) copy-start(f32[768]{0:T(1024)} %param.18) | copy-start | bytes 9220
  9.7 1.4 copy-start.9
  11.1 0.9 copy-start.4
  14.1 0.8 copy-start.3
  16.0 1.5 copy-start.5
  17.8 20.2 %copy-start.13 = (f32[768]{0:T(1024)S(1)}, f32[768]{0:T(1024)}, u32[]{:S(2)}) copy-start(f32[768]{0:T(1024)} %param.22) | copy-start | bytes 9220
  38.0 1.4 copy-start.1
  40.9 1.8 %copy-start.15 = (f32[768]{0:T(1024)S(1)}, f32[768]{0:T(1024)}, u32[]{:S(2)}) copy-start(f32[768]{0:T(1024)} %param.23) | copy-start | bytes 9220
  40.9 1.8 %copy-start.18 = (f32[768]{0:T(1024)S(1)}, f32[768]{0:T(1024)}, u32[]{:S(2)}) copy-start(f32[768]{0:T(1024)} %param.24) | copy-start | bytes 9220
  42.7 0.7 copy-start.21
  43.3 1.1 copy-start.10
  43.3 1.5 copy-start.20
  53.2 107.8 %copy-start.2 = (f32[2,208,768]{2,1,0:T(8,128)S(1)}, f32[2,208,768]{2,1,0:T(8,128)}, u32[]{:S(2)}) copy-start(f32[2,208,768]{2,1,0:T(8,128)} %get-tuple-element.76) | copy-start | bytes 3833860
  53.2 107.8 %copy-start.19 = (f32[768]{0:T(1024)S(1)}, f32[768]{0:T(1024)}, u32[]{:S(2)}) copy-start(f32[768]{0:T(1024)} %param.28) | copy-start | bytes 9220
  161.0 2.6 %copy-start.16 = (f32[16,768]{1,0:T(8,128)S(1)}, f32[16,768]{1,0:T(8,128)}, u32[]{:S(2)}) copy-start(f32[16,768]{1,0:T(8,128)} %get-tuple-element.22) | copy-start | bytes 147460
  162.3 2.6 %copy-start.8 = (bf16[4,8,24,768]{3,2,1,0:T(8,128)(2,1)S(1)}, bf16[4,8,24,768]{3,2,1,0:T(8,128)(2,1)}, u32[]{:S(2)}) copy-start(bf16[4,8,24,768]{3,2,1,0:T(8,128)(2,1)} %get-tuple-element.23) | copy-start | bytes 3538948
  165.0 1.2 copy-start.12
  167.5 1.6 copy-start.6
  167.5 2.3 %copy-start.7 = (bf16[3,8,32,768]{3,2,1,0:T(8,128)(2,1)S(1)}, bf16[3,8,32,768]{3,2,1,0:T(8,128)(2,1)}, u32[]{:S(2)}) copy-start(bf16[3,8,32,768]{3,2,1,0:T(8,128)(2,1)} %get-tuple-element.25) | copy-start | bytes 3538948
